TPU v7x, 32 devices: a whole 2x2x4 slice. The times are simulated.
32 devices in a mesh: ctx: 4 (over z), exp: 8 (over y, x, core).
Axes of the slice: x: 2, y: 2, z: 4, core: 2. Of those that a mesh axis runs over, the one named last changes fastest.
Arguments:
- out_grad: bfloat16 [4096, 2048], P(('ctx', 'exp')), may hold values from -6 to 6
- route_ids: int32 [4096, 4], P(('ctx', 'exp')), may hold values from 0 to 15, all different within a row; in each aligned block of 128 rows (0 to 127, 128 to 255, ...) at most 36 rows name the same one
- gate_probs: float32 [4096, 4], P(('ctx', 'exp')), may hold values from 0 to 1, as said below
- saved_hidden: bfloat16 [4, 8, 16, 36, 768], P('ctx', None, 'exp'), may hold values from -6 to 6
- down_weight: bfloat16 [16, 768, 2048], P('exp', None, 'ctx'), may hold values from -0.02734375 to 0.02734375
- router_weight: bfloat16 [2048, 16], replicated, may hold values from -1.5 to 1.5
- proj_weight: bfloat16 [4096, 2048], P('ctx'), may hold values from -0.125 to 0.125
Outputs:
- head_grads: bfloat16 [4, 1024, 4096], P(None, 'exp', 'ctx')
- router_grad: float32 [4096, 4], P(('ctx', 'exp'))
Inputs may be any that keep to these rules, and one draw needn't show every extreme that they name: `route_ids`: each token names 4 different experts; among the tokens of one device no expert is named more than 36 times, and in some device some expert is named exactly 36 times. `gate_probs`: positive; a token's 4 gates sum to one.
All inputs are finite; a program needn't handle non-finite values.
Results may differ from a plain program's by a relative error of at most 0.009.
Values may be sent and summed in bfloat16 or wider, within the bound.
A program may use at most 64 MiB of HBM per device.

v0:
```python
import jax
import jax.numpy as jnp
from jax import lax
from jax.sharding import PartitionSpec as P


def route_ranks(route_ids, experts):
    flat_ids = route_ids.reshape(-1)
    onehot = (flat_ids[:, None] == jnp.arange(experts, dtype=jnp.int32)[None, :]).astype(jnp.int32)
    earlier = jnp.cumsum(onehot, axis=0) - onehot
    slot_rank = jnp.sum(earlier * onehot, axis=1)
    return (flat_ids, slot_rank)


def shards(out_grad, route_ids, gate_probs, saved_hidden, down_weight, router_weight, proj_weight):
    tok_rows, top_count = route_ids.shape
    experts = router_weight.shape[1]
    groups = lax.axis_size("exp")
    n_ctx = lax.axis_size("ctx")
    local_experts = down_weight.shape[0]
    capacity = saved_hidden.shape[3]
    dslice = down_weight.shape[2]
    me_ctx = lax.axis_index("ctx")
    rows_all = lax.all_gather(out_grad, "ctx", axis=0, tiled=False)
    packed = jnp.concatenate([route_ids.astype(jnp.float32), gate_probs], axis=1)
    packed_all = lax.all_gather(packed, "ctx", axis=0, tiled=False)
    ids_all = packed_all[:, :, :top_count].astype(jnp.int32)
    probs_all = packed_all[:, :, top_count:]
    own = saved_hidden[0]
    right, left, from_left, from_right = (own, own, [], [])
    for _ in range(n_ctx - 1):
        right = lax.ppermute(right, "ctx", [(i, i + 1) for i in range(n_ctx - 1)])
        left = lax.ppermute(left, "ctx", [(i + 1, i) for i in range(n_ctx - 1)])
        from_left.append(right)
        from_right.append(left)
    hidden_all = jnp.zeros((n_ctx,) + own.shape, own.dtype)
    for k in range(n_ctx - 1, 0, -1):
        hidden_all = lax.dynamic_update_index_in_dim(
            hidden_all, from_left[k - 1], jnp.maximum(me_ctx - k, 0), 0
        )
    for k in range(n_ctx - 1, 0, -1):
        hidden_all = lax.dynamic_update_index_in_dim(
            hidden_all, from_right[k - 1], jnp.minimum(me_ctx + k, n_ctx - 1), 0
        )
    hidden_all = lax.dynamic_update_index_in_dim(hidden_all, own, me_ctx, 0)
    flat_ids, slot_rank = jax.vmap(lambda r: route_ranks(r, experts))(ids_all)
    positions = flat_ids * capacity + slot_rank
    cols = lax.dynamic_slice_in_dim(rows_all, me_ctx * dslice, dslice, axis=2)
    spread = jnp.repeat(cols, top_count, axis=1)
    blk = jnp.broadcast_to(jnp.arange(n_ctx, dtype=jnp.int32)[:, None], flat_ids.shape)
    send_rows = (
        jnp.zeros((groups, n_ctx, local_experts, capacity, dslice), out_grad.dtype)
        .at[flat_ids // local_experts, blk, flat_ids % local_experts, slot_rank]
        .set(spread)
    )
    arrived = lax.all_to_all(send_rows, "exp", split_axis=0, concat_axis=0, tiled=True)
    outputs = jnp.einsum(
        "csekf,efn->scekn", hidden_all, down_weight, preferred_element_type=jnp.float32
    ).astype(jnp.bfloat16)
    partial_grad = jnp.sum(arrived.astype(jnp.float32) * outputs.astype(jnp.float32), axis=4)
    returned = lax.all_to_all(partial_grad, "exp", split_axis=0, concat_axis=0, tiled=True)
    returned = lax.psum(returned, "ctx")
    returned = jnp.transpose(returned, (1, 0, 2, 3)).reshape(n_ctx, experts * capacity)
    picks = positions[:, :, None] == jnp.arange(experts * capacity, dtype=jnp.int32)[None, None, :]
    gate_grad = jnp.sum(jnp.where(picks, returned[:, None, :], 0.0), axis=2)
    gate_grad = gate_grad.reshape(n_ctx, tok_rows, top_count)
    weighted = jnp.sum(probs_all * gate_grad, axis=2, keepdims=True)
    router_all = probs_all * (gate_grad - weighted)
    matches = ids_all[:, :, :, None] == jnp.arange(experts, dtype=jnp.int32)[None, None, None, :]
    dense_all = jnp.sum(jnp.where(matches, router_all[:, :, :, None], 0.0), axis=2)
    router_wide = router_weight.astype(jnp.float32)
    combined = (
        rows_all.astype(jnp.float32)
        + lax.dot_general(
            dense_all, router_wide, (((2,), (1,)), ((), ())), precision=lax.Precision.HIGHEST
        )
    ).astype(jnp.bfloat16)
    head_flat = lax.dot_general(
        combined.reshape(n_ctx * tok_rows, -1),
        proj_weight,
        (((1,), (1,)), ((), ())),
        preferred_element_type=jnp.float32,
    ).astype(jnp.bfloat16)
    head_grads = head_flat.reshape(n_ctx, tok_rows, proj_weight.shape[0])
    router_grad = lax.dynamic_index_in_dim(router_all, me_ctx, axis=0, keepdims=False)
    return (head_grads, router_grad)


def solution(mesh):
    return jax.shard_map(
        shards,
        mesh=mesh,
        in_specs=(
            P(("ctx", "exp"), None),
            P(("ctx", "exp"), None),
            P(("ctx", "exp"), None),
            P("ctx", None, "exp", None, None),
            P("exp", None, "ctx"),
            P(),
            P("ctx", None),
        ),
        out_specs=(P(None, "exp", "ctx"), P(("ctx", "exp"), None)),
        check_vma=False,
    )
```

profile of v0, /device:TPU:0, one launch (start us, length us, event | category | flops | bytes accessed | tf_op | source)
XLA Modules:
  0.0 219.9 jit_solution(10738357573883738285)
XLA Ops:
  7.9 5.9 %collective-permute-start = (bf16[8,2,36,768]{3,1,2,0:T(2,128)(2,1)}, bf16[8,2,36,768]{3,1,2,0:T(2,128)(2,1)}, u32[]{:S(2)}, u32[]{:S(2)}) collective-permute-start(bf16[8,2,36,768]{3,1,2,0:T(2,128)(2,1)} %bitcast.61), channel_id=1, source_target_pairs={{0,8},{8,16},{16,24},{1,9},{9,17},{17,25},{2,10},{10,18},{18,26},{... | collective-permute-start | bytes 2654216 | tf_op jit(solution)/shard_map/ppermute | solution.py:32
  13.8 1.3 collective-permute-start.3
  15.1 29.6 %collective-permute-done = bf16[8,2,36,768]{3,1,2,0:T(2,128)(2,1)} collective-permute-done((bf16[8,2,36,768]{3,1,2,0:T(2,128)(2,1)}, bf16[8,2,36,768]{3,1,2,0:T(2,128)(2,1)}, u32[]{:S(2)}, u32[]{:S(2)}) %collective-permute-start) | collective-permute-done | bytes 884768 | tf_op jit(solution)/shard_map/ppermute | solution.py:32
  44.6 15.3 %collective-permute-start.1 = (bf16[8,2,36,768]{3,1,2,0:T(2,128)(2,1)}, bf16[8,2,36,768]{3,1,2,0:T(2,128)(2,1)}, u32[]{:S(2)}, u32[]{:S(2)}) collective-permute-start(bf16[8,2,36,768]{3,1,2,0:T(2,128)(2,1)} %collective-permute-done), channel_id=1, source_target_pairs={{0,8},{8,16},{16,24},{1,9},{9,17},{17,25},{2,10},{10,18},{18,26},{... | collective-permute-start | bytes 2654216 | tf_op jit(solution)/shard_map/ppermute | solution.py:32
  61.3 31.7 %all-gather.1 = f32[512,8]{0,1:T(8,128)S(1)} all-gather(f32[128,8]{0,1:T(8,128)S(1)} %pad_maximum_fusion), channel_id=3, replica_groups=mesh['ctx'=4,'exp'=8] {'ctx'}, dimensions={0}, use_global_device_ids=true | all-gather | bytes 20480 | tf_op jit(solution)/shard_map/all_gather | solution.py:26
  93.8 4.6 %reduce-window.6 = s32[4,16,4,128]{3,1,2,0:T(8,128)S(1)} reduce-window(s32[4,16,4,128]{3,1,2,0:T(8,128)S(1)} %fusion.7, s32[]{:T(128)} %constant.71.clone.1), window={size=1x1x1x128 pad=0_0x0_0x0_0x127_0}, to_apply=%region_0.1 | reduce-window | flops 4161536 | bytes 262148 | tf_op jit(solution)/shard_map/reduce-window
  99.0 1.3 collective-permute-start.4
  100.3 5.5 %collective-permute-start.2 = (bf16[8,2,36,768]{3,1,2,0:T(2,128)(2,1)}, bf16[8,2,36,768]{3,1,2,0:T(2,128)(2,1)}, u32[]{:S(2)}, u32[]{:S(2)}) collective-permute-start(bf16[8,2,36,768]{3,1,2,0:T(2,128)(2,1)} %collective-permute-done.1), channel_id=1, source_target_pairs={{0,8},{8,16},{16,24},{1,9},{9,17},{17,25},{2,10},{10,18},{18,26},{... | collective-permute-start | bytes 2654216 | tf_op jit(solution)/shard_map/ppermute | solution.py:32
  106.5 0.7 and_reduce_fusion
  107.3 1.1 constant_dynamic-slice_fusion.1
  108.4 1.9 broadcast_in_dim.74
  110.3 4.0 %reshape.204 = bf16[2048,512]{1,0:T(8,128)(2,1)} reshape(bf16[4,128,4,512]{3,2,1,0:T(4,128)(2,1)} %broadcast_in_dim.74) | data formatting | bytes 4194304 | tf_op jit(solution)/shard_map/reshape | solution.py:49
  114.3 11.6 %scatter_custom_fusion = bf16[2304,512]{1,0:T(8,128)(2,1)} fusion(s32[2048]{0:T(1024)S(1)} %bitcast.65, bf16[2048,512]{1,0:T(8,128)(2,1)} %reshape.204, bf16[]{:T(256)} %constant.72.clone.1), kind=kCustom, calls=%fused_computation.8 | custom fusion | bytes 2359808
  125.9 5.9 %reshape.200 = bf16[8,4,36,2,512]{4,3,2,1,0:T(2,128)(2,1)} reshape(bf16[2304,512]{1,0:T(8,128)(2,1)} %scatter_custom_fusion) | data formatting | bytes 4718592
  131.8 4.3 %copy.69 = bf16[8,4,2,36,512]{4,1,3,2,0:T(4,128)(2,1)} copy(bf16[8,4,2,36,512]{4,2,3,1,0:T(2,128)(2,1)} %bitcast.54) | data formatting | bytes 4718592 | tf_op jit(solution)/shard_map/scatter | solution.py:54
  136.1 4.4 %all-to-all-start = ((bf16[8,4,2,36,512]{4,1,3,2,0:T(4,128)(2,1)}), bf16[8,4,2,36,512]{4,1,3,2,0:T(4,128)(2,1)}, u32[]{:S(2)}, u32[]{:S(2)}) async-start(bf16[8,4,2,36,512]{4,1,3,2,0:T(4,128)(2,1)} %copy.69), calls=%async_computation | async-start | bytes 4718592 | tf_op jit(solution)/shard_map/all_to_all | solution.py:56
  140.5 1.5 collective-permute-start.5
  142.0 2.1 broadcast_in_dim.75
  144.2 2.2 %copy_dynamic-update-slice_fusion.6 = bf16[4,8,2,36,768]{4,3,1,0,2:T(8,128)(2,1)} fusion(bf16[4,8,2,36,768]{4,3,1,0,2:T(8,128)(2,1)} %broadcast_in_dim.75, s32[]{:T(128)S(6)} %max.9, bf16[1,8,2,36,768]{4,2,3,1,0:T(2,128)(2,1)} %bitcast.6), kind=kLoop, calls=%fused_computation.16 | loop fusion | bytes 1867780 | tf_op jit(solution)/shard_map/jit(dynamic_update_index_in_dim)/dynamic_update_slice | solution.py:38
  146.4 2.2 %copy_dynamic-update-slice_fusion.5 = bf16[4,8,2,36,768]{4,3,1,0,2:T(8,128)(2,1)} fusion(bf16[4,8,2,36,768]{4,3,1,0,2:T(8,128)(2,1)} %copy_dynamic-update-slice_fusion.6, s32[]{:T(128)S(6)} %max.10, bf16[1,8,2,36,768]{4,2,3,1,0:T(2,128)(2,1)} %bitcast.7), kind=kLoop, calls=%fused_computation.15 | loop fusion | bytes 1867780 | tf_op jit(solution)/shard_map/jit(dynamic_update_index_in_dim)/dynamic_update_slice | solution.py:38
  148.6 2.3 %copy_dynamic-update-slice_fusion.4 = bf16[4,8,2,36,768]{4,3,1,0,2:T(8,128)(2,1)} fusion(bf16[4,8,2,36,768]{4,3,1,0,2:T(8,128)(2,1)} %copy_dynamic-update-slice_fusion.5, s32[]{:T(128)S(6)} %max.11, bf16[1,8,2,36,768]{4,2,3,1,0:T(2,128)(2,1)} %bitcast.8), kind=kLoop, calls=%fused_computation.14 | loop fusion | bytes 1867780 | tf_op jit(solution)/shard_map/jit(dynamic_update_index_in_dim)/dynamic_update_slice | solution.py:38
  151.0 13.7 %collective-permute-done.5 = bf16[8,2,36,768]{3,1,2,0:T(2,128)(2,1)} collective-permute-done((bf16[8,2,36,768]{3,1,2,0:T(2,128)(2,1)}, bf16[8,2,36,768]{3,1,2,0:T(2,128)(2,1)}, u32[]{:S(2)}, u32[]{:S(2)}) %collective-permute-start.5) | collective-permute-done | bytes 884768 | tf_op jit(solution)/shard_map/ppermute | solution.py:33
  164.7 2.2 %copy_dynamic-update-slice_fusion.3 = bf16[4,8,2,36,768]{4,3,1,0,2:T(8,128)(2,1)} fusion(bf16[4,8,2,36,768]{4,3,1,0,2:T(8,128)(2,1)} %copy_dynamic-update-slice_fusion.4, s32[]{:T(128)S(6)} %select_n.93, bf16[1,8,2,36,768]{4,2,3,1,0:T(2,128)(2,1)} %bitcast.9), kind=kLoop, calls=%fused_computation.13 | loop fusion | bytes 1867780 | tf_op jit(solution)/shard_map/jit(dynamic_update_index_in_dim)/dynamic_update_slice | solution.py:42
  166.9 2.2 %copy_dynamic-update-slice_fusion.2 = bf16[4,8,2,36,768]{4,3,1,0,2:T(8,128)(2,1)} fusion(bf16[4,8,2,36,768]{4,3,1,0,2:T(8,128)(2,1)} %copy_dynamic-update-slice_fusion.3, s32[]{:T(128)S(6)} %select_n.94, bf16[1,8,2,36,768]{4,2,3,1,0:T(2,128)(2,1)} %bitcast.10), kind=kLoop, calls=%fused_computation.12 | loop fusion | bytes 1867780 | tf_op jit(solution)/shard_map/jit(dynamic_update_index_in_dim)/dynamic_update_slice | solution.py:42
  169.1 1.1 copy_dynamic-update-slice_fusion.1
  170.2 1.1 copy_dynamic-update-slice_fusion
  171.3 5.6 %fusion = f32[8,4,2,36]{3,0,1,2:T(8,128)S(1)} fusion(bf16[8,4,2,36,512]{4,1,3,2,0:T(4,128)(2,1)} %all-to-all-done, bf16[4,8,2,36,768]{4,3,1,0,2:T(8,128)(2,1)} %copy_dynamic-update-slice_fusion, bf16[2,768,512]{2,1,0:T(8,128)(2,1)S(1)} %copy-done), kind=kOutput, calls=%fused_computation.2 | convolution fusion | flops 1817835264 | bytes 7480320 | tf_op jit(solution)/shard_map/csekf,efn->scekn/dot_general | solution.py:57
  177.6 3.8 %all-to-all-start.1 = ((f32[8,1,288]{2,1,0:T(1,128)}), f32[8,1,288]{2,1,0:T(1,128)S(1)}, u32[]{:S(2)}, u32[]{:S(2)}) async-start(f32[8,1,288]{2,1,0:T(1,128)} %reshape.216), calls=%async_computation.1 | async-start | bytes 24576 | tf_op jit(solution)/shard_map/all_to_all | solution.py:61
  181.6 4.6 %all-to-all-done.1 = f32[8,1,288]{2,1,0:T(1,128)S(1)} async-done(((f32[8,1,288]{2,1,0:T(1,128)}), f32[8,1,288]{2,1,0:T(1,128)S(1)}, u32[]{:S(2)}, u32[]{:S(2)}) %all-to-all-start.1) | async-done | bytes 9248 | tf_op jit(solution)/shard_map/all_to_all | solution.py:61
  187.6 16.1 %psum.7 = f32[4,576]{1,0:T(4,128)S(1)} all-reduce(f32[4,576]{1,0:T(4,128)S(1)} %broadcast_in_dim.82), channel_id=1, replica_groups=mesh['ctx'=4,'exp'=8] {'ctx'}, use_global_device_ids=true, to_apply=%region_5.6 | all-reduce | flops 2304 | bytes 18432 | tf_op jit(solution)/shard_map/psum | solution.py:62
  206.0 3.7 %add_convert_fusion = bf16[4,128,2048]{2,1,0:T(8,128)(2,1)S(1)} fusion(bf16[4,128,2048]{2,1,0:T(8,128)(2,1)} %bitcast.59, f32[4,128,16]{1,2,0:T(8,128)S(1)} %select_reduce_fusion.1, bf16[2048,16]{0,1:T(8,128)(2,1)S(1)} %copy-done.2), kind=kOutput, calls=%fused_computation.5 | convolution fusion | flops 204472320 | bytes 4292608 | tf_op jit(solution)/shard_map/dot_general | solution.py:74
  209.7 3.3 %convolution_convert_fusion = bf16[512,1024]{1,0:T(8,128)(2,1)} fusion(bf16[512,2048]{1,0:T(8,128)(2,1)S(1)} %bitcast.60, bf16[1024,2048]{1,0:T(8,128)(2,1)S(1)} %copy-done.3), kind=kOutput, calls=%fused_computation.7 | convolution fusion | flops 2148007936 | bytes 7340032 | tf_op jit(solution)/shard_map/dot_general | solution.py:78
  (50 shorter events, 8.7 us)
Async XLA Ops:
  7.2 164.1 %copy-start = (bf16[2,768,512]{2,1,0:T(8,128)(2,1)S(1)}, bf16[2,768,512]{2,1,0:T(8,128)(2,1)}, u32[]{:S(2)}) copy-start(bf16[2,768,512]{2,1,0:T(8,128)(2,1)} %param.11) | copy-start | bytes 4718596
  7.2 100.1 %all-gather.4.cloned.1.call-start = ((), (), s32[]{:S(2)}) async-start(), calls=%async_computation.2 | async-start | bytes 2621440 | tf_op jit(solution)/shard_map/all_gather | solution.py:24
  7.9 36.7 %collective-permute-start = (bf16[8,2,36,768]{3,1,2,0:T(2,128)(2,1)}, bf16[8,2,36,768]{3,1,2,0:T(2,128)(2,1)}, u32[]{:S(2)}, u32[]{:S(2)}) collective-permute-start(bf16[8,2,36,768]{3,1,2,0:T(2,128)(2,1)} %bitcast.61), channel_id=1, source_target_pairs={{0,8},{8,16},{16,24},{1,9},{9,17},{17,25},{2,10},{10,18},{18,26},{... | collective-permute-start | bytes 2654216 | tf_op jit(solution)/shard_map/ppermute | solution.py:32
  13.8 85.1 %collective-permute-start.3 = (bf16[8,2,36,768]{3,1,2,0:T(2,128)(2,1)}, bf16[8,2,36,768]{3,1,2,0:T(2,128)(2,1)S(1)}, u32[]{:S(2)}, u32[]{:S(2)}) collective-permute-start(bf16[8,2,36,768]{3,1,2,0:T(2,128)(2,1)} %bitcast.62), channel_id=1, source_target_pairs={{8,0},{16,8},{24,16},{9,1},{17,9},{25,17},{10,2},{18,10},{26,18},{... | collective-permute-start | bytes 2654216 | tf_op jit(solution)/shard_map/ppermute | solution.py:33
  44.6 55.6 %collective-permute-start.1 = (bf16[8,2,36,768]{3,1,2,0:T(2,128)(2,1)}, bf16[8,2,36,768]{3,1,2,0:T(2,128)(2,1)}, u32[]{:S(2)}, u32[]{:S(2)}) collective-permute-start(bf16[8,2,36,768]{3,1,2,0:T(2,128)(2,1)} %collective-permute-done), channel_id=1, source_target_pairs={{0,8},{8,16},{16,24},{1,9},{9,17},{17,25},{2,10},{10,18},{18,26},{... | collective-permute-start | bytes 2654216 | tf_op jit(solution)/shard_map/ppermute | solution.py:32
  99.0 41.6 %collective-permute-start.4 = (bf16[8,2,36,768]{3,1,2,0:T(2,128)(2,1)S(1)}, bf16[8,2,36,768]{3,1,2,0:T(2,128)(2,1)}, u32[]{:S(2)}, u32[]{:S(2)}) collective-permute-start(bf16[8,2,36,768]{3,1,2,0:T(2,128)(2,1)S(1)} %collective-permute-done.3), channel_id=1, source_target_pairs={{8,0},{16,8},{24,16},{9,1},{17,9},{25,17},{10,2},{18,10},{26,18},{... | collective-permute-start | bytes 2654216 | tf_op jit(solution)/shard_map/ppermute | solution.py:33
  100.3 41.8 %collective-permute-start.2 = (bf16[8,2,36,768]{3,1,2,0:T(2,128)(2,1)}, bf16[8,2,36,768]{3,1,2,0:T(2,128)(2,1)}, u32[]{:S(2)}, u32[]{:S(2)}) collective-permute-start(bf16[8,2,36,768]{3,1,2,0:T(2,128)(2,1)} %collective-permute-done.1), channel_id=1, source_target_pairs={{0,8},{8,16},{16,24},{1,9},{9,17},{17,25},{2,10},{10,18},{18,26},{... | collective-permute-start | bytes 2654216 | tf_op jit(solution)/shard_map/ppermute | solution.py:32
  136.1 35.1 %all-to-all-start = ((bf16[8,4,2,36,512]{4,1,3,2,0:T(4,128)(2,1)}), bf16[8,4,2,36,512]{4,1,3,2,0:T(4,128)(2,1)}, u32[]{:S(2)}, u32[]{:S(2)}) async-start(bf16[8,4,2,36,512]{4,1,3,2,0:T(4,128)(2,1)} %copy.69), calls=%async_computation | async-start | bytes 4718592 | tf_op jit(solution)/shard_map/all_to_all | solution.py:56
  140.5 24.1 %collective-permute-start.5 = (bf16[8,2,36,768]{3,1,2,0:T(2,128)(2,1)}, bf16[8,2,36,768]{3,1,2,0:T(2,128)(2,1)}, u32[]{:S(2)}, u32[]{:S(2)}) collective-permute-start(bf16[8,2,36,768]{3,1,2,0:T(2,128)(2,1)} %collective-permute-done.4), channel_id=1, source_target_pairs={{8,0},{16,8},{24,16},{9,1},{17,9},{25,17},{10,2},{18,10},{26,18},{... | collective-permute-start | bytes 2654216 | tf_op jit(solution)/shard_map/ppermute | solution.py:33
  148.6 21.5 %copy-start.1 = (bf16[1,8,2,36,768]{4,2,3,1,0:T(2,128)(2,1)S(1)}, bf16[1,8,2,36,768]{4,2,3,1,0:T(2,128)(2,1)}, u32[]{:S(2)}) copy-start(bf16[1,8,2,36,768]{4,2,3,1,0:T(2,128)(2,1)} %param.10) | copy-start | bytes 2654212
  171.2 34.7 %copy-start.2 = (bf16[2048,16]{0,1:T(8,128)(2,1)S(1)}, bf16[2048,16]{0,1:T(8,128)(2,1)}, u32[]{:S(2)}) copy-start(bf16[2048,16]{0,1:T(8,128)(2,1)} %param.12) | copy-start | bytes 196612
  177.6 8.6 %all-to-all-start.1 = ((f32[8,1,288]{2,1,0:T(1,128)}), f32[8,1,288]{2,1,0:T(1,128)S(1)}, u32[]{:S(2)}, u32[]{:S(2)}) async-start(f32[8,1,288]{2,1,0:T(1,128)} %reshape.216), calls=%async_computation.1 | async-start | bytes 24576 | tf_op jit(solution)/shard_map/all_to_all | solution.py:61
  206.0 3.7 %copy-start.3 = (bf16[1024,2048]{1,0:T(8,128)(2,1)S(1)}, bf16[1024,2048]{1,0:T(8,128)(2,1)}, u32[]{:S(2)}) copy-start(bf16[1024,2048]{1,0:T(8,128)(2,1)} %param.13) | copy-start | bytes 12582916
Sparse Core Ops, SparseCore 0:
  9.6 66.6 all-gather.3
where the time goes:
time: 221 us; the launch traced here: 220 us
  waiting for transfers between devices  48.6 us (22%)
  local copies, waits for them, and re-layouts  48 us (22%)
  blocking collectives  47.8 us (22%)
  starting transfers between devices  39 us (18%)
  between operations  14.3 us (6%)
  matrix products  12.6 us (6%)
  other arithmetic  9.51 us (4%)
    all_gather x1, blocking collectives, shards(): packed_all = lax.all_gather(packed, 'ctx', axis=0, tiled=False)  31.7 us
    ppermute x3, waiting for transfers between devices, shards(): right = lax.ppermute(right, 'ctx', [(i, i + 1) for i in range(n_ctx - 1)])  29.6 us
    ppermute x3, starting transfers between devices, shards(): right = lax.ppermute(right, 'ctx', [(i, i + 1) for i in range(n_ctx - 1)])  26.7 us
    unnamed x13, local copies, waits for them, and re-layouts  18.4 us
    psum x1, blocking collectives, shards(): returned = lax.psum(returned, 'ctx')  16.1 us
    ppermute x3, waiting for transfers between devices, shards(): left = lax.ppermute(left, 'ctx', [(i + 1, i) for i in range(n_ctx - 1)])  13.7 us
    dynamic_update_slice x3, local copies, waits for them, and re-layouts, shards(): lax.dynamic_update_index_in_dim(hidden_all, from_left[k - 1], jnp.maximum...  6.78 us
    dot_general x1, matrix products, shards(): jnp.einsum('csekf,efn->scekn', hidden_all, down_weight, preferred_element...  5.59 us
  transfers between devices with their start and end apart: 9, of which 3 were waited for; matrix products, arithmetic and copies ran while one was open for 24% of the time, Pallas kernels for 0%

commit v1 on v0

--- a/solution.py
+++ b/solution.py
@@ -59,7 +59,7 @@
     ).astype(jnp.bfloat16)
     partial_grad = jnp.sum(arrived.astype(jnp.float32) * outputs.astype(jnp.float32), axis=4)
     returned = lax.all_to_all(partial_grad, "exp", split_axis=0, concat_axis=0, tiled=True)
-    returned = lax.psum(returned, "ctx")
+    returned = jnp.sum(lax.all_gather(returned, "ctx"), axis=0)
     returned = jnp.transpose(returned, (1, 0, 2, 3)).reshape(n_ctx, experts * capacity)
     picks = positions[:, :, None] == jnp.arange(experts * capacity, dtype=jnp.int32)[None, None, :]
     gate_grad = jnp.sum(jnp.where(picks, returned[:, None, :], 0.0), axis=2)

time: 221 us -> 218 us (0.986)
  blocking collectives: 47.8 us -> 45.1 us
    psum x1 -> x0, blocking collectives: 16.1 us -> none  [shards(): returned = lax.psum(returned, 'ctx')]
    all_gather x0 -> x1, blocking collectives: none -> 13.4 us  [shards(): returned = jnp.sum(lax.all_gather(returned, 'ctx'), axis=0)]
where the time goes in v1:
time: 218 us; the launch traced here: 217 us
  waiting for transfers between devices  48.6 us (22%)
  local copies, waits for them, and re-layouts  48 us (22%)
  blocking collectives  45.1 us (21%)
  starting transfers between devices  39 us (18%)
  between operations  14.3 us (7%)
  matrix products  12.6 us (6%)
  other arithmetic  9.55 us (4%)
    all_gather x1, blocking collectives, shards(): packed_all = lax.all_gather(packed, 'ctx', axis=0, tiled=False)  31.7 us
    ppermute x3, waiting for transfers between devices, shards(): right = lax.ppermute(right, 'ctx', [(i, i + 1) for i in range(n_ctx - 1)])  29.6 us
    ppermute x3, starting transfers between devices, shards(): right = lax.ppermute(right, 'ctx', [(i, i + 1) for i in range(n_ctx - 1)])  26.7 us
    unnamed x13, local copies, waits for them, and re-layouts  18.4 us
    ppermute x3, waiting for transfers between devices, shards(): left = lax.ppermute(left, 'ctx', [(i + 1, i) for i in range(n_ctx - 1)])  13.7 us
    all_gather x1, blocking collectives, shards(): returned = jnp.sum(lax.all_gather(returned, 'ctx'), axis=0)  13.4 us
    dynamic_update_slice x3, local copies, waits for them, and re-layouts, shards(): lax.dynamic_update_index_in_dim(hidden_all, from_left[k - 1], jnp.maximum...  6.78 us
    dot_general x1, matrix products, shards(): jnp.einsum('csekf,efn->scekn', hidden_all, down_weight, preferred_element...  5.59 us
  transfers between devices with their start and end apart: 9, of which 3 were waited for; matrix products, arithmetic and copies ran while one was open for 24% of the time, Pallas kernels for 0%

profile of v1, /device:TPU:0, one launch (start us, length us, event | category | flops | bytes accessed | tf_op | source)
XLA Modules:
  0.0 217.2 jit_solution(12404448526780112093)
XLA Ops:
  7.9 5.9 %collective-permute-start = (bf16[8,2,36,768]{3,1,2,0:T(2,128)(2,1)}, bf16[8,2,36,768]{3,1,2,0:T(2,128)(2,1)}, u32[]{:S(2)}, u32[]{:S(2)}) collective-permute-start(bf16[8,2,36,768]{3,1,2,0:T(2,128)(2,1)} %bitcast.66), channel_id=1, source_target_pairs={{0,8},{8,16},{16,24},{1,9},{9,17},{17,25},{2,10},{10,18},{18,26},{... | collective-permute-start | bytes 2654216 | tf_op jit(solution)/shard_map/ppermute | solution.py:32
  13.8 1.3 collective-permute-start.3
  15.1 29.6 %collective-permute-done = bf16[8,2,36,768]{3,1,2,0:T(2,128)(2,1)} collective-permute-done((bf16[8,2,36,768]{3,1,2,0:T(2,128)(2,1)}, bf16[8,2,36,768]{3,1,2,0:T(2,128)(2,1)}, u32[]{:S(2)}, u32[]{:S(2)}) %collective-permute-start) | collective-permute-done | bytes 884768 | tf_op jit(solution)/shard_map/ppermute | solution.py:32
  44.6 15.3 %collective-permute-start.1 = (bf16[8,2,36,768]{3,1,2,0:T(2,128)(2,1)}, bf16[8,2,36,768]{3,1,2,0:T(2,128)(2,1)}, u32[]{:S(2)}, u32[]{:S(2)}) collective-permute-start(bf16[8,2,36,768]{3,1,2,0:T(2,128)(2,1)} %collective-permute-done), channel_id=1, source_target_pairs={{0,8},{8,16},{16,24},{1,9},{9,17},{17,25},{2,10},{10,18},{18,26},{... | collective-permute-start | bytes 2654216 | tf_op jit(solution)/shard_map/ppermute | solution.py:32
  61.3 31.7 %all-gather.1 = f32[512,8]{0,1:T(8,128)S(1)} all-gather(f32[128,8]{0,1:T(8,128)S(1)} %pad_maximum_fusion), channel_id=3, replica_groups=mesh['ctx'=4,'exp'=8] {'ctx'}, dimensions={0}, use_global_device_ids=true | all-gather | bytes 20480 | tf_op jit(solution)/shard_map/all_gather | solution.py:26
  93.8 4.6 %reduce-window.6 = s32[4,16,4,128]{3,1,2,0:T(8,128)S(1)} reduce-window(s32[4,16,4,128]{3,1,2,0:T(8,128)S(1)} %fusion.7, s32[]{:T(128)} %constant.71.clone.1), window={size=1x1x1x128 pad=0_0x0_0x0_0x127_0}, to_apply=%region_0.1 | reduce-window | flops 4161536 | bytes 262148 | tf_op jit(solution)/shard_map/reduce-window
  99.0 1.3 collective-permute-start.4
  100.3 5.5 %collective-permute-start.2 = (bf16[8,2,36,768]{3,1,2,0:T(2,128)(2,1)}, bf16[8,2,36,768]{3,1,2,0:T(2,128)(2,1)}, u32[]{:S(2)}, u32[]{:S(2)}) collective-permute-start(bf16[8,2,36,768]{3,1,2,0:T(2,128)(2,1)} %collective-permute-done.1), channel_id=1, source_target_pairs={{0,8},{8,16},{16,24},{1,9},{9,17},{17,25},{2,10},{10,18},{18,26},{... | collective-permute-start | bytes 2654216 | tf_op jit(solution)/shard_map/ppermute | solution.py:32
  106.5 0.7 and_reduce_fusion
  107.3 1.1 constant_dynamic-slice_fusion.1
  108.4 1.9 broadcast_in_dim.74
  110.3 4.0 %reshape.204 = bf16[2048,512]{1,0:T(8,128)(2,1)} reshape(bf16[4,128,4,512]{3,2,1,0:T(4,128)(2,1)} %broadcast_in_dim.74) | data formatting | bytes 4194304 | tf_op jit(solution)/shard_map/reshape | solution.py:49
  114.3 11.6 %scatter_custom_fusion = bf16[2304,512]{1,0:T(8,128)(2,1)} fusion(s32[2048]{0:T(1024)S(1)} %bitcast.73, bf16[2048,512]{1,0:T(8,128)(2,1)} %reshape.204, bf16[]{:T(256)} %constant.72.clone.1), kind=kCustom, calls=%fused_computation.8 | custom fusion | bytes 2359808
  125.9 5.9 %reshape.200 = bf16[8,4,36,2,512]{4,3,2,1,0:T(2,128)(2,1)} reshape(bf16[2304,512]{1,0:T(8,128)(2,1)} %scatter_custom_fusion) | data formatting | bytes 4718592
  131.8 4.3 %copy.82 = bf16[8,4,2,36,512]{4,1,3,2,0:T(4,128)(2,1)} copy(bf16[8,4,2,36,512]{4,2,3,1,0:T(2,128)(2,1)} %bitcast.59) | data formatting | bytes 4718592 | tf_op jit(solution)/shard_map/scatter | solution.py:54
  136.1 4.4 %all-to-all-start = ((bf16[8,4,2,36,512]{4,1,3,2,0:T(4,128)(2,1)}), bf16[8,4,2,36,512]{4,1,3,2,0:T(4,128)(2,1)}, u32[]{:S(2)}, u32[]{:S(2)}) async-start(bf16[8,4,2,36,512]{4,1,3,2,0:T(4,128)(2,1)} %copy.82), calls=%async_computation | async-start | bytes 4718592 | tf_op jit(solution)/shard_map/all_to_all | solution.py:56
  140.5 1.5 collective-permute-start.5
  142.0 2.1 broadcast_in_dim.75
  144.2 2.2 %copy_dynamic-update-slice_fusion.6 = bf16[4,8,2,36,768]{4,3,1,0,2:T(8,128)(2,1)} fusion(bf16[4,8,2,36,768]{4,3,1,0,2:T(8,128)(2,1)} %broadcast_in_dim.75, s32[]{:T(128)S(6)} %max.9, bf16[1,8,2,36,768]{4,2,3,1,0:T(2,128)(2,1)} %bitcast.6), kind=kLoop, calls=%fused_computation.16 | loop fusion | bytes 1867780 | tf_op jit(solution)/shard_map/jit(dynamic_update_index_in_dim)/dynamic_update_slice | solution.py:38
  146.4 2.2 %copy_dynamic-update-slice_fusion.5 = bf16[4,8,2,36,768]{4,3,1,0,2:T(8,128)(2,1)} fusion(bf16[4,8,2,36,768]{4,3,1,0,2:T(8,128)(2,1)} %copy_dynamic-update-slice_fusion.6, s32[]{:T(128)S(6)} %max.10, bf16[1,8,2,36,768]{4,2,3,1,0:T(2,128)(2,1)} %bitcast.7), kind=kLoop, calls=%fused_computation.15 | loop fusion | bytes 1867780 | tf_op jit(solution)/shard_map/jit(dynamic_update_index_in_dim)/dynamic_update_slice | solution.py:38
  148.6 2.3 %copy_dynamic-update-slice_fusion.4 = bf16[4,8,2,36,768]{4,3,1,0,2:T(8,128)(2,1)} fusion(bf16[4,8,2,36,768]{4,3,1,0,2:T(8,128)(2,1)} %copy_dynamic-update-slice_fusion.5, s32[]{:T(128)S(6)} %max.11, bf16[1,8,2,36,768]{4,2,3,1,0:T(2,128)(2,1)} %bitcast.8), kind=kLoop, calls=%fused_computation.14 | loop fusion | bytes 1867780 | tf_op jit(solution)/shard_map/jit(dynamic_update_index_in_dim)/dynamic_update_slice | solution.py:38
  151.0 13.7 %collective-permute-done.5 = bf16[8,2,36,768]{3,1,2,0:T(2,128)(2,1)} collective-permute-done((bf16[8,2,36,768]{3,1,2,0:T(2,128)(2,1)}, bf16[8,2,36,768]{3,1,2,0:T(2,128)(2,1)}, u32[]{:S(2)}, u32[]{:S(2)}) %collective-permute-start.5) | collective-permute-done | bytes 884768 | tf_op jit(solution)/shard_map/ppermute | solution.py:33
  164.7 2.2 %copy_dynamic-update-slice_fusion.3 = bf16[4,8,2,36,768]{4,3,1,0,2:T(8,128)(2,1)} fusion(bf16[4,8,2,36,768]{4,3,1,0,2:T(8,128)(2,1)} %copy_dynamic-update-slice_fusion.4, s32[]{:T(128)S(6)} %select_n.93, bf16[1,8,2,36,768]{4,2,3,1,0:T(2,128)(2,1)} %bitcast.9), kind=kLoop, calls=%fused_computation.13 | loop fusion | bytes 1867780 | tf_op jit(solution)/shard_map/jit(dynamic_update_index_in_dim)/dynamic_update_slice | solution.py:42
  166.9 2.2 %copy_dynamic-update-slice_fusion.2 = bf16[4,8,2,36,768]{4,3,1,0,2:T(8,128)(2,1)} fusion(bf16[4,8,2,36,768]{4,3,1,0,2:T(8,128)(2,1)} %copy_dynamic-update-slice_fusion.3, s32[]{:T(128)S(6)} %select_n.94, bf16[1,8,2,36,768]{4,2,3,1,0:T(2,128)(2,1)} %bitcast.10), kind=kLoop, calls=%fused_computation.12 | loop fusion | bytes 1867780 | tf_op jit(solution)/shard_map/jit(dynamic_update_index_in_dim)/dynamic_update_slice | solution.py:42
  169.1 1.1 copy_dynamic-update-slice_fusion.1
  170.2 1.1 copy_dynamic-update-slice_fusion
  171.3 5.6 %fusion = f32[8,4,2,36]{3,0,1,2:T(8,128)S(1)} fusion(bf16[8,4,2,36,512]{4,1,3,2,0:T(4,128)(2,1)} %all-to-all-done, bf16[4,8,2,36,768]{4,3,1,0,2:T(8,128)(2,1)} %copy_dynamic-update-slice_fusion, bf16[2,768,512]{2,1,0:T(8,128)(2,1)S(1)} %copy-done), kind=kOutput, calls=%fused_computation.2 | convolution fusion | flops 1817835264 | bytes 7480320 | tf_op jit(solution)/shard_map/csekf,efn->scekn/dot_general | solution.py:57
  177.6 3.8 %all-to-all-start.1 = ((f32[8,1,288]{2,1,0:T(1,128)}), f32[8,1,288]{2,1,0:T(1,128)S(1)}, u32[]{:S(2)}, u32[]{:S(2)}) async-start(f32[8,1,288]{2,1,0:T(1,128)} %reshape.217), calls=%async_computation.1 | async-start | bytes 24576 | tf_op jit(solution)/shard_map/all_to_all | solution.py:61
  181.5 4.6 %all-to-all-done.1 = f32[8,1,288]{2,1,0:T(1,128)S(1)} async-done(((f32[8,1,288]{2,1,0:T(1,128)}), f32[8,1,288]{2,1,0:T(1,128)S(1)}, u32[]{:S(2)}, u32[]{:S(2)}) %all-to-all-start.1) | async-done | bytes 9248 | tf_op jit(solution)/shard_map/all_to_all | solution.py:61
  187.4 13.4 %all-gather.2 = f32[32,4,2,36]{3,1,2,0:T(4,128)S(1)} all-gather(f32[8,4,2,36]{3,1,2,0:T(4,128)S(1)} %bitcast.71), channel_id=4, replica_groups=mesh['ctx'=4,'exp'=8] {'ctx'}, dimensions={0}, use_global_device_ids=true | all-gather | bytes 46080 | tf_op jit(solution)/shard_map/all_gather | solution.py:62
  203.3 3.7 %add_convert_fusion = bf16[4,128,2048]{2,1,0:T(8,128)(2,1)S(1)} fusion(bf16[4,128,2048]{2,1,0:T(8,128)(2,1)} %bitcast.64, f32[4,128,16]{1,2,0:T(8,128)S(1)} %select_reduce_fusion.1, bf16[2048,16]{0,1:T(8,128)(2,1)S(1)} %copy-done.2), kind=kOutput, calls=%fused_computation.5 | convolution fusion | flops 204472320 | bytes 4292608 | tf_op jit(solution)/shard_map/dot_general | solution.py:74
  207.0 3.3 %convolution_convert_fusion = bf16[512,1024]{1,0:T(8,128)(2,1)} fusion(bf16[512,2048]{1,0:T(8,128)(2,1)S(1)} %bitcast.65, bf16[1024,2048]{1,0:T(8,128)(2,1)S(1)} %copy-done.3), kind=kOutput, calls=%fused_computation.7 | convolution fusion | flops 2148007936 | bytes 7340032 | tf_op jit(solution)/shard_map/dot_general | solution.py:78
  (51 shorter events, 8.7 us)
Async XLA Ops:
  7.2 164.1 %copy-start = (bf16[2,768,512]{2,1,0:T(8,128)(2,1)S(1)}, bf16[2,768,512]{2,1,0:T(8,128)(2,1)}, u32[]{:S(2)}) copy-start(bf16[2,768,512]{2,1,0:T(8,128)(2,1)} %param.11) | copy-start | bytes 4718596
  7.2 100.1 %all-gather.5.cloned.1.call-start = ((), (), s32[]{:S(2)}) async-start(), calls=%async_computation.2 | async-start | bytes 2621440 | tf_op jit(solution)/shard_map/all_gather | solution.py:24
  7.9 36.7 %collective-permute-start = (bf16[8,2,36,768]{3,1,2,0:T(2,128)(2,1)}, bf16[8,2,36,768]{3,1,2,0:T(2,128)(2,1)}, u32[]{:S(2)}, u32[]{:S(2)}) collective-permute-start(bf16[8,2,36,768]{3,1,2,0:T(2,128)(2,1)} %bitcast.66), channel_id=1, source_target_pairs={{0,8},{8,16},{16,24},{1,9},{9,17},{17,25},{2,10},{10,18},{18,26},{... | collective-permute-start | bytes 2654216 | tf_op jit(solution)/shard_map/ppermute | solution.py:32
  13.8 85.1 %collective-permute-start.3 = (bf16[8,2,36,768]{3,1,2,0:T(2,128)(2,1)}, bf16[8,2,36,768]{3,1,2,0:T(2,128)(2,1)S(1)}, u32[]{:S(2)}, u32[]{:S(2)}) collective-permute-start(bf16[8,2,36,768]{3,1,2,0:T(2,128)(2,1)} %bitcast.67), channel_id=1, source_target_pairs={{8,0},{16,8},{24,16},{9,1},{17,9},{25,17},{10,2},{18,10},{26,18},{... | collective-permute-start | bytes 2654216 | tf_op jit(solution)/shard_map/ppermute | solution.py:33
  44.6 55.6 %collective-permute-start.1 = (bf16[8,2,36,768]{3,1,2,0:T(2,128)(2,1)}, bf16[8,2,36,768]{3,1,2,0:T(2,128)(2,1)}, u32[]{:S(2)}, u32[]{:S(2)}) collective-permute-start(bf16[8,2,36,768]{3,1,2,0:T(2,128)(2,1)} %collective-permute-done), channel_id=1, source_target_pairs={{0,8},{8,16},{16,24},{1,9},{9,17},{17,25},{2,10},{10,18},{18,26},{... | collective-permute-start | bytes 2654216 | tf_op jit(solution)/shard_map/ppermute | solution.py:32
  99.0 41.6 %collective-permute-start.4 = (bf16[8,2,36,768]{3,1,2,0:T(2,128)(2,1)S(1)}, bf16[8,2,36,768]{3,1,2,0:T(2,128)(2,1)}, u32[]{:S(2)}, u32[]{:S(2)}) collective-permute-start(bf16[8,2,36,768]{3,1,2,0:T(2,128)(2,1)S(1)} %collective-permute-done.3), channel_id=1, source_target_pairs={{8,0},{16,8},{24,16},{9,1},{17,9},{25,17},{10,2},{18,10},{26,18},{... | collective-permute-start | bytes 2654216 | tf_op jit(solution)/shard_map/ppermute | solution.py:33
  100.3 41.8 %collective-permute-start.2 = (bf16[8,2,36,768]{3,1,2,0:T(2,128)(2,1)}, bf16[8,2,36,768]{3,1,2,0:T(2,128)(2,1)}, u32[]{:S(2)}, u32[]{:S(2)}) collective-permute-start(bf16[8,2,36,768]{3,1,2,0:T(2,128)(2,1)} %collective-permute-done.1), channel_id=1, source_target_pairs={{0,8},{8,16},{16,24},{1,9},{9,17},{17,25},{2,10},{10,18},{18,26},{... | collective-permute-start | bytes 2654216 | tf_op jit(solution)/shard_map/ppermute | solution.py:32
  136.1 35.1 %all-to-all-start = ((bf16[8,4,2,36,512]{4,1,3,2,0:T(4,128)(2,1)}), bf16[8,4,2,36,512]{4,1,3,2,0:T(4,128)(2,1)}, u32[]{:S(2)}, u32[]{:S(2)}) async-start(bf16[8,4,2,36,512]{4,1,3,2,0:T(4,128)(2,1)} %copy.82), calls=%async_computation | async-start | bytes 4718592 | tf_op jit(solution)/shard_map/all_to_all | solution.py:56
  140.5 24.1 %collective-permute-start.5 = (bf16[8,2,36,768]{3,1,2,0:T(2,128)(2,1)}, bf16[8,2,36,768]{3,1,2,0:T(2,128)(2,1)}, u32[]{:S(2)}, u32[]{:S(2)}) collective-permute-start(bf16[8,2,36,768]{3,1,2,0:T(2,128)(2,1)} %collective-permute-done.4), channel_id=1, source_target_pairs={{8,0},{16,8},{24,16},{9,1},{17,9},{25,17},{10,2},{18,10},{26,18},{... | collective-permute-start | bytes 2654216 | tf_op jit(solution)/shard_map/ppermute | solution.py:33
  148.6 21.5 %copy-start.1 = (bf16[1,8,2,36,768]{4,2,3,1,0:T(2,128)(2,1)S(1)}, bf16[1,8,2,36,768]{4,2,3,1,0:T(2,128)(2,1)}, u32[]{:S(2)}) copy-start(bf16[1,8,2,36,768]{4,2,3,1,0:T(2,128)(2,1)} %param.10) | copy-start | bytes 2654212
  171.2 32.0 %copy-start.2 = (bf16[2048,16]{0,1:T(8,128)(2,1)S(1)}, bf16[2048,16]{0,1:T(8,128)(2,1)}, u32[]{:S(2)}) copy-start(bf16[2048,16]{0,1:T(8,128)(2,1)} %param.12) | copy-start | bytes 196612
  177.6 8.6 %all-to-all-start.1 = ((f32[8,1,288]{2,1,0:T(1,128)}), f32[8,1,288]{2,1,0:T(1,128)S(1)}, u32[]{:S(2)}, u32[]{:S(2)}) async-start(f32[8,1,288]{2,1,0:T(1,128)} %reshape.217), calls=%async_computation.1 | async-start | bytes 24576 | tf_op jit(solution)/shard_map/all_to_all | solution.py:61
  203.3 3.7 %copy-start.3 = (bf16[1024,2048]{1,0:T(8,128)(2,1)S(1)}, bf16[1024,2048]{1,0:T(8,128)(2,1)}, u32[]{:S(2)}) copy-start(bf16[1024,2048]{1,0:T(8,128)(2,1)} %param.13) | copy-start | bytes 12582916
Sparse Core Ops, SparseCore 0:
  9.6 66.6 all-gather.4
